TPU v7x, 128 devices: a whole 4x4x4 slice. The times are simulated.
128 devices in a mesh: tensor: 8 (over y, core), adapter: 16 (over x, z).
Axes of the slice: x: 4, y: 4, z: 4, core: 2. Of those that a mesh axis runs over, the one named last changes fastest.
Arguments:
- tokens_in: bfloat16 [512, 8192], P(('tensor', 'adapter')), may hold values from -6 to 6
- w_gate: bfloat16 [8192, 28672], P(None, ('tensor', 'adapter')), may hold values from -0.0625 to 0.0625
- w_up: bfloat16 [8192, 28672], P(None, ('tensor', 'adapter')), may hold values from -0.0625 to 0.0625
- w_down: bfloat16 [28672, 8192], P('tensor', 'adapter'), may hold values from -0.03125 to 0.03125
- a_gate: bfloat16 [8192, 2048], P(None, 'adapter'), may hold values from -0.0625 to 0.0625
- a_up: bfloat16 [8192, 2048], P(None, 'adapter'), may hold values from -0.0625 to 0.0625
- b_gate: bfloat16 [2048, 28672], P(None, ('tensor', 'adapter')), may hold values from -1.5 to 1.5
- b_up: bfloat16 [2048, 28672], P(None, ('tensor', 'adapter')), may hold values from -1.5 to 1.5
- a_down: bfloat16 [28672, 2048], P(('tensor', 'adapter')), may hold values from -0.03125 to 0.03125
- b_down: bfloat16 [2048, 8192], P('adapter'), may hold values from -1.5 to 1.5
- lengths: int32 [8], replicated, may hold values from 1 to 128, 512 in all
- request_adapter: int32 [8], replicated, may hold values from 0 to 127
- placement: int32 [128], replicated, may hold values from 0 to 127, each once
Outputs:
- mixed: bfloat16 [512, 8192], P(('tensor', 'adapter'))
Inputs may be any that keep to these rules, and one draw needn't show every extreme that they name: The 8 lengths sum to 512; the longest is exactly 512 // 4. `placement`: each storage slot holds exactly one adapter.
All inputs are finite; a program needn't handle non-finite values.
Results may differ from a plain program's by a relative error of at most 0.0085.
Values may be sent and summed in bfloat16 or wider, within the bound.
No kernel may reach another device: no remote copies, remote signals or barrier semaphores. Data moves between devices by JAX's collectives and lax.ppermute only.
A program may use at most 128 MiB of HBM per device.

v0:
```python
import jax
import jax.numpy as jnp
from jax import lax
from jax.sharding import PartitionSpec as P

R = 16
ADP_DEV = 8


def token_tables(lengths, request_adapter, placement, all_tokens):
    positions = jnp.arange(all_tokens, dtype=jnp.int32)
    request_ends = jnp.cumsum(lengths)
    request = jnp.sum((positions[:, None] >= request_ends[None, :]).astype(jnp.int32), axis=1)
    request_hot = request[:, None] == jnp.arange(lengths.shape[0], dtype=jnp.int32)[None, :]
    adapter = jnp.sum(jnp.where(request_hot, request_adapter[None, :], 0), axis=1)
    adapter_hot = adapter[:, None] == jnp.arange(placement.shape[0], dtype=jnp.int32)[None, :]
    slot_index = jnp.sum(jnp.where(adapter_hot, placement[None, :], 0), axis=1)
    return (adapter_hot, slot_index)


def spread_block(low_rank, hot_rows):
    spread = jnp.where(
        hot_rows[:, :, None], low_rank[:, None, :], jnp.zeros_like(low_rank)[:, None, :]
    )
    return spread.reshape(low_rank.shape[0], -1)


def owner_shrink(rows_in, a_gate, a_up):
    return jnp.concatenate(
        [
            jnp.dot(rows_in, a_gate, preferred_element_type=jnp.float32),
            jnp.dot(rows_in, a_up, preferred_element_type=jnp.float32),
        ],
        axis=1,
    )


def local(
    tokens_in,
    w_gate,
    w_up,
    w_down,
    a_gate,
    a_up,
    b_gate,
    b_up,
    a_down,
    b_down,
    lengths,
    request_adapter,
    placement,
):
    n_tensor = lax.axis_size("tensor")
    n_adapter = lax.axis_size("adapter")
    tok_dev = tokens_in.shape[0]
    all_tokens = tok_dev * n_tensor * n_adapter
    group_rows = tok_dev * n_adapter
    adapter_count = placement.shape[0]
    adapter_hot, slot_index = token_tables(lengths, request_adapter, placement, all_tokens)
    group_start = lax.axis_index("tensor") * group_rows
    group_slot = lax.dynamic_slice_in_dim(slot_index, group_start, group_rows)
    owned = group_slot // ADP_DEV == lax.axis_index("adapter")
    local_mask = (group_slot % ADP_DEV)[:, None] == jnp.arange(ADP_DEV, dtype=jnp.int32)[None, :]
    keep_mask = owned[:, None] & local_mask
    rows_group = lax.all_gather(tokens_in, "adapter", axis=0, tiled=True)
    projected = owner_shrink(rows_group, a_gate, a_up).reshape(group_rows, 2, ADP_DEV, R)
    picked = jnp.sum(jnp.where(keep_mask[:, None, :, None], projected, 0.0), axis=2).reshape(
        group_rows, 2 * R
    )
    shrunk_group = lax.psum(picked, "adapter").astype(jnp.bfloat16)
    gathered, shrunk_all = (
        lax.all_gather(rows_group, "tensor", axis=0, tiled=True),
        lax.all_gather(shrunk_group, "tensor", axis=0, tiled=True),
    )
    gate_sum = jnp.dot(gathered, w_gate, preferred_element_type=jnp.float32) + jnp.dot(
        spread_block(shrunk_all[:, :R], adapter_hot), b_gate, preferred_element_type=jnp.float32
    )
    up_sum = jnp.dot(gathered, w_up, preferred_element_type=jnp.float32) + jnp.dot(
        spread_block(shrunk_all[:, R:], adapter_hot), b_up, preferred_element_type=jnp.float32
    )
    hidden = (jax.nn.silu(gate_sum) * up_sum).astype(jnp.bfloat16)
    down_all = jnp.dot(hidden, a_down, preferred_element_type=jnp.float32).reshape(
        all_tokens, adapter_count, R
    )
    low_part = jnp.sum(jnp.where(adapter_hot[:, :, None], down_all, 0.0), axis=1)
    down_full = lax.all_to_all(w_down, "adapter", split_axis=0, concat_axis=1, tiled=True)
    base_part = jnp.dot(hidden, down_full, preferred_element_type=jnp.float32)
    base_sum, low_sum = (
        lax.psum_scatter(base_part, ("tensor", "adapter"), scatter_dimension=0, tiled=True),
        lax.psum_scatter(low_part, ("tensor", "adapter"), scatter_dimension=0, tiled=True),
    )
    low_rank = low_sum.astype(jnp.bfloat16)
    low_group = lax.all_gather(low_rank, "adapter", axis=0, tiled=True)
    spread_low = jnp.where(
        keep_mask[:, :, None], low_group[:, None, :], jnp.zeros_like(low_group)[:, None, :]
    )
    spread_low = spread_low.reshape(group_rows, ADP_DEV * R)
    expanded = jnp.dot(spread_low, b_down, preferred_element_type=jnp.float32).astype(jnp.bfloat16)
    delta_down = lax.psum_scatter(
        expanded.astype(jnp.float32).astype(jnp.bfloat16),
        "adapter",
        scatter_dimension=0,
        tiled=True,
    ).astype(jnp.float32)
    return (base_sum + delta_down).astype(jnp.bfloat16)


def solution(mesh):
    in_specs = (
        P(("tensor", "adapter"), None),
        P(None, ("tensor", "adapter")),
        P(None, ("tensor", "adapter")),
        P("tensor", "adapter"),
        P(None, "adapter"),
        P(None, "adapter"),
        P(None, ("tensor", "adapter")),
        P(None, ("tensor", "adapter")),
        P(("tensor", "adapter"), None),
        P("adapter", None),
        P(),
        P(),
        P(),
    )
    out_specs = P(("tensor", "adapter"), None)
    return jax.shard_map(local, mesh=mesh, in_specs=in_specs, out_specs=out_specs, check_vma=False)
```

profile of v0, /device:TPU:1, one launch (start us, length us, event | category | flops | bytes accessed | tf_op | source)
XLA Modules:
  0.0 604.1 jit_solution(13579343601903260206)
XLA Ops:
  6.5 0.7 all-gather.8.cloned.1.call-update
  7.3 0.0 all-gather.6.cloned.1.call-start
  7.3 46.2 %all-gather.8.cloned.1.call-done = bf16[16,4,8192]{2,1,0:T(4,128)(2,1)} async-done(((bf16[1,4,8192]{2,1,0:T(4,128)(2,1)}), bf16[16,4,8192]{2,1,0:T(4,128)(2,1)}) %all-gather.8.cloned.1.call-update) | async-done | bytes 1048592 | tf_op jit(solution)/shard_map/all_gather | solution.py:65
  53.5 2.1 reshape.155
  55.7 0.0 all-gather.6.cloned.1.call-update
  55.7 0.0 copy-start.11
  55.7 0.0 copy-start.6
  55.7 0.0 copy-start.7
  55.8 4.7 all-to-all-start
  60.4 0.0 all-reduce.8.cloned.1.call-start
  60.5 0.2 reduce-window.8
  60.7 0.1 convert_reduce_fusion
  60.8 0.1 select_reduce_fusion.3
  60.9 0.1 select_reduce_fusion.1
  61.0 0.1 fusion.5
  61.1 2.1 fusion.8
  63.2 2.1 fusion.9
  65.3 0.1 copy.29
  65.5 90.2 %psum.7 = bf16[64,32]{0,1:T(8,128)(2,1)S(1)} all-reduce(f32[64,32]{0,1:T(8,128)S(1)} %bitcast.47), channel_id=1, replica_groups=mesh['tensor'=8,'adapter'=16] {'adapter'}, use_global_device_ids=true, to_apply=%region_5.6 | all-reduce | flops 2048 | bytes 12288 | tf_op jit(solution)/shard_map/psum | solution.py:70
  155.6 28.5 %all-gather.1 = bf16[8,64,32]{1,2,0:T(8,128)(2,1)S(1)} all-gather(bf16[1,64,32]{1,2,0:T(8,128)(2,1)S(1)} %bitcast.50), channel_id=1, replica_groups=mesh['tensor'=8,'adapter'=16] {'tensor'}, dimensions={0}, use_global_device_ids=true | all-gather | bytes 36864 | tf_op jit(solution)/shard_map/all_gather | solution.py:73
  184.2 0.1 reshape.157
  184.3 2.4 broadcast_select_fusion.1
  186.7 7.2 %fusion.7 = f32[512,224]{0,1:T(8,128)S(1)} fusion(bf16[512,8192]{1,0:T(8,128)(2,1)} %all-gather.6.cloned.1.call-done, bf16[8192,224]{0,1:T(8,128)(2,1)} %param.14), kind=kOutput, calls=%fused_computation.31 | convolution fusion | flops 1879048192 | bytes 12517376 | tf_op jit(solution)/shard_map/dot_general | solution.py:75
  194.0 0.0 copy-start.9
  194.0 0.6 convolution_add_fusion.1
  194.7 1.5 copy-done.9
  196.2 2.7 fusion.10
  198.8 0.0 copy-start.5
  198.9 0.7 fusion.1
  199.5 0.5 copy-done.5
  200.0 0.8 fusion.12
  200.8 0.9 select_reduce_fusion
  201.6 0.1 copy.33
  201.8 65.0 %all-reduce.1 = bf16[512,16]{1,0:T(8,128)(2,1)S(1)} all-reduce(f32[512,16]{1,0:T(8,128)S(1)} %copy.33), channel_id=3, replica_groups=mesh['tensor'=8,'adapter'=16] {'tensor','adapter'}, use_global_device_ids=true, to_apply=%region_8.9.clone | all-reduce | flops 8192 | bytes 49152
  266.8 16.0 %all-gather.2 = bf16[16,4,16]{2,1,0:T(4,128)(2,1)S(1)} all-gather(bf16[1,4,16]{2,1,0:T(4,128)(2,1)S(1)} %fusion.4), channel_id=1, replica_groups=mesh['tensor'=8,'adapter'=16] {'adapter'}, dimensions={0}, use_global_device_ids=true | all-gather | bytes 2176 | tf_op jit(solution)/shard_map/all_gather | solution.py:93
  282.8 0.1 copy.34
  282.9 1.5 convolution_convert_fusion
  284.4 0.0 all-reduce.8.cloned.1.call-update
  284.4 0.0 all-reduce.6.cloned.1.call-start
  284.4 0.0 all-to-all-done
  284.4 2.4 copy.36
  286.9 8.1 %fusion.11 = f32[512,8192]{1,0:T(8,128)} fusion(bf16[512,224]{0,1:T(8,128)(2,1)S(1)} %fusion.1, bf16[224,8192]{1,0:T(8,128)(2,1)S(1)} %bitcast.41), kind=kOutput, calls=%fused_computation.35 | convolution fusion | flops 1879048192 | bytes 20676608 | tf_op jit(solution)/shard_map/dot_general | solution.py:87
  295.0 0.0 all-reduce.6.cloned.1.call-update
  295.0 0.6 copy-done.12
  295.6 0.6 dynamic-slice.2
  296.9 76.9 %all-reduce.8.cloned.1.call-done = bf16[64,8192]{1,0:T(8,128)(2,1)} async-done(((bf16[64,8192]{1,0:T(8,128)(2,1)}), bf16[64,8192]{1,0:T(8,128)(2,1)}) %all-reduce.8.cloned.1.call-update) | async-done | bytes 1048592
  373.8 222.0 %all-reduce.6.cloned.1.call-done = f32[512,8192]{1,0:T(8,128)} async-done(((f32[512,8192]{1,0:T(8,128)}), f32[512,8192]{1,0:T(8,128)}) %all-reduce.6.cloned.1.call-update) | async-done | bytes 16777232
  595.9 1.7 fusion.2
  (29 shorter events, 0.2 us)
Async XLA Ops:
  6.5 276.3 %copy-start = (bf16[128,8192]{1,0:T(8,128)(2,1)S(1)}, bf16[128,8192]{1,0:T(8,128)(2,1)}, u32[]{:S(2)}) copy-start(bf16[128,8192]{1,0:T(8,128)(2,1)} %param.22) | copy-start | bytes 6291460
  6.5 47.0 %all-gather.8.cloned.1.call-start = ((), (), s32[]{:S(2)}) async-start(), calls=%async_computation.2 | async-start | bytes 1114112 | tf_op jit(solution)/shard_map/all_gather | solution.py:65
  7.3 179.5 %all-gather.6.cloned.1.call-start = ((), (), s32[]{:S(2)}) async-start(), calls=%async_computation.1 | async-start | bytes 9437184 | tf_op jit(solution)/shard_map/all_gather | solution.py:72
  55.7 4.8 copy-start.11
  55.7 5.0 copy-start.6
  55.7 5.1 copy-start.7
  55.7 5.4 copy-start.1
  55.8 228.7 %all-to-all-start = ((bf16[16,224,512]{2,1,0:T(8,128)(2,1)}), bf16[16,224,512]{2,1,0:T(8,128)(2,1)}, u32[]{:S(2)}, u32[]{:S(2)}) async-start(bf16[16,224,512]{2,1,0:T(8,128)(2,1)} %bitcast.43), calls=%async_computation | async-start | bytes 7340032 | tf_op jit(solution)/shard_map/all_to_all | solution.py:86
  60.4 313.4 %all-reduce.8.cloned.1.call-start = ((), (), s32[]{:S(2)}) async-start(), calls=%async_computation.4 | async-start | bytes 2097152
  186.7 7.3 %copy-start.4 = (bf16[2048,224]{0,1:T(8,128)(2,1)S(1)}, bf16[2048,224]{0,1:T(8,128)(2,1)}, u32[]{:S(2)}) copy-start(bf16[2048,224]{0,1:T(8,128)(2,1)} %param.19) | copy-start | bytes 2752516
  186.7 7.3 %copy-start.2 = (bf16[512,128,16]{0,2,1:T(8,128)(2,1)S(1)}, bf16[512,128,16]{0,2,1:T(8,128)(2,1)}, u32[]{:S(2)}) copy-start(bf16[512,128,16]{0,2,1:T(8,128)(2,1)} %get-tuple-element.7) | copy-start | bytes 6291460
  186.7 7.9 %copy-start.8 = (bf16[512,8192]{1,0:T(8,128)(2,1)S(1)}, bf16[512,8192]{1,0:T(8,128)(2,1)}, u32[]{:S(2)}) copy-start(bf16[512,8192]{1,0:T(8,128)(2,1)} %all-gather.6.cloned.1.call-done) | copy-start | bytes 25165828
  194.0 2.2 copy-start.9
  196.2 2.7 copy-start.3
  196.2 2.7 copy-start.10
  198.8 1.2 copy-start.5
  284.4 311.5 %all-reduce.6.cloned.1.call-start = ((), (), s32[]{:S(2)}) async-start(), calls=%async_computation.3 | async-start | bytes 33554432
  295.0 0.7 copy-start.12
Sparse Core Ops, SparseCore 0:
  9.5 44.0 all-gather.7
  55.8 51.1 all-gather.5
  284.5 89.2 all-reduce.7
  379.1 216.7 all-reduce.5
where the time goes:
time: 605 us; the launch traced here: 604 us
  waiting for transfers between devices  346 us (57%)
  blocking collectives  200 us (33%)
  matrix products  25.7 us (4%)
  between operations  14.1 us (2%)
  local copies, waits for them, and re-layouts  8.25 us (1%)
    unnamed x6, waiting for transfers between devices  300 us
    psum x1, blocking collectives, local(): shrunk_group = lax.psum(picked, 'adapter').astype(jnp.bfloat16)  90.2 us
    unnamed x1, blocking collectives  65 us
    all_gather x1, waiting for transfers between devices, local(): rows_group = lax.all_gather(tokens_in, 'adapter', axis=0, tiled=True)  46.2 us
    all_gather x1, blocking collectives, local(): lax.all_gather(shrunk_group, 'tensor', axis=0, tiled=True)  28.5 us
    all_gather x1, blocking collectives, local(): low_group = lax.all_gather(low_rank, 'adapter', axis=0, tiled=True)  16 us
  transfers between devices with their start and end apart: 5, of which 3 were waited for; matrix products, arithmetic and copies ran while one was open for 5% of the time, Pallas kernels for 0%

commit v1 on v0

--- a/solution.py
+++ b/solution.py
@@ -68,9 +68,34 @@
         group_rows, 2 * R
     )
     shrunk_group = lax.psum(picked, "adapter").astype(jnp.bfloat16)
+
+    def points_settle(piece_in):
+        a_next = jax.lax.axis_size("tensor")
+        m_next = jax.lax.axis_index("tensor")
+        v_now, answer, w_next = (a_next, m_next, piece_in.shape[0])
+        gallery = list(map(lambda src_i: (src_i, (src_i + 1) % v_now), range(v_now)))
+        vals = list(map(lambda src_i: (src_i, (src_i - 1) % v_now), range(v_now)))
+        finding = jnp.zeros(
+            (*piece_in.shape[:0], v_now * w_next, *piece_in.shape[1:]), piece_in.dtype
+        )
+        finding = lax.dynamic_update_slice_in_dim(finding, piece_in, answer * w_next, axis=0)
+        side_arr = now = piece_in
+        tmp = v_now // 2
+        for i0 in range(1, tmp + 1):
+            side_arr = jax.lax.ppermute(side_arr, "tensor", gallery)
+            finding = lax.dynamic_update_slice_in_dim(
+                finding, side_arr, (answer - i0) % v_now * w_next, axis=0
+            )
+            if i0 < v_now - tmp:
+                now = jax.lax.ppermute(now, "tensor", vals)
+                finding = lax.dynamic_update_slice_in_dim(
+                    finding, now, (answer + i0) % v_now * w_next, axis=0
+                )
+        return finding
+
     gathered, shrunk_all = (
         lax.all_gather(rows_group, "tensor", axis=0, tiled=True),
-        lax.all_gather(shrunk_group, "tensor", axis=0, tiled=True),
+        points_settle(shrunk_group),
     )
     gate_sum = jnp.dot(gathered, w_gate, preferred_element_type=jnp.float32) + jnp.dot(
         spread_block(shrunk_all[:, :R], adapter_hot), b_gate, preferred_element_type=jnp.float32

time: 605 us -> 594 us (0.982)
  blocking collectives: 200 us -> 158 us
  starting transfers between devices: 4.78 us -> 28.2 us
    psum x1, blocking collectives: 90.2 us -> 57.9 us  [local(): shrunk_group = lax.psum(picked, 'adapter').astype(jnp.bfloat16)]
    all_gather x1 -> x0, blocking collectives: 28.5 us -> none  [local(): lax.all_gather(shrunk_group, 'tensor', axis=0, tiled=True)]
    ppermute x0 -> x7, starting transfers between devices: none -> 23.5 us  [the longest x4 22.4 us: points_settle(): side_arr = jax.lax.ppermute(side_arr, 'tensor', gallery)]
    unnamed x1, blocking collectives: 65 us -> 83.3 us
  transfers between devices with their start and end apart: 5 -> 12, of which waited for: 3 -> 7; matrix products, arithmetic and copies ran while one was open for 5% -> 6% of each run, Pallas kernels for 0% -> 0%
where the time goes in v1:
time: 594 us; the launch traced here: 593 us
  waiting for transfers between devices  349 us (59%)
  blocking collectives  158 us (27%)
  starting transfers between devices  28.2 us (5%)
  matrix products  26.1 us (4%)
  between operations  14.1 us (2%)
  local copies, waits for them, and re-layouts  9.88 us (2%)
  other arithmetic  7.63 us (1%)
    unnamed x6, waiting for transfers between devices  299 us
    unnamed x1, blocking collectives  83.3 us
    psum x1, blocking collectives, local(): shrunk_group = lax.psum(picked, 'adapter').astype(jnp.bfloat16)  57.9 us
    all_gather x1, waiting for transfers between devices, local(): rows_group = lax.all_gather(tokens_in, 'adapter', axis=0, tiled=True)  46.2 us
    ppermute x4, starting transfers between devices, points_settle(): side_arr = jax.lax.ppermute(side_arr, 'tensor', gallery)  22.4 us
    all_gather x1, blocking collectives, local(): low_group = lax.all_gather(low_rank, 'adapter', axis=0, tiled=True)  17.2 us
  transfers between devices with their start and end apart: 12, of which 7 were waited for; matrix products, arithmetic and copies ran while one was open for 6% of the time, Pallas kernels for 0%

profile of v1, /device:TPU:1, one launch (start us, length us, event | category | flops | bytes accessed | tf_op | source)
XLA Modules:
  0.0 593.3 jit_solution(7147196665726780806)
XLA Ops:
  6.5 0.7 all-gather.7.cloned.1.call-update
  7.3 46.2 %all-gather.7.cloned.1.call-done = bf16[16,4,8192]{2,1,0:T(4,128)(2,1)} async-done(((bf16[1,4,8192]{2,1,0:T(4,128)(2,1)}), bf16[16,4,8192]{2,1,0:T(4,128)(2,1)}) %all-gather.7.cloned.1.call-update) | async-done | bytes 1048592 | tf_op jit(solution)/shard_map/all_gather | solution.py:65
  53.5 2.1 reshape.155
  55.7 0.9 reduce-window.8
  56.7 0.7 select_reduce_fusion.3
  57.5 0.8 select_reduce_fusion.1
  58.3 2.4 fusion.8
  60.8 2.1 fusion.9
  63.0 57.9 %psum.7 = bf16[64,32]{0,1:T(8,128)(2,1)S(1)} all-reduce(f32[64,32]{0,1:T(8,128)S(1)} %bitcast.42), channel_id=1, replica_groups=mesh['tensor'=8,'adapter'=16] {'adapter'}, use_global_device_ids=true, to_apply=%region_5.6 | all-reduce | flops 2048 | bytes 12288 | tf_op jit(solution)/shard_map/psum | solution.py:70
  120.8 17.8 %collective-permute-start = (bf16[64,32]{0,1:T(8,128)(2,1)S(1)}, bf16[64,32]{0,1:T(8,128)(2,1)S(1)}, u32[]{:S(2)}, u32[]{:S(2)}) collective-permute-start(bf16[64,32]{0,1:T(8,128)(2,1)S(1)} %psum.7), channel_id=1, source_target_pairs={{0,16},{16,32},{32,48},{48,64},{64,80},{80,96},{96,112},{112,0},{1... | collective-permute-start | bytes 12296 | tf_op jit(solution)/shard_map/ppermute | solution.py:85
  138.6 0.8 collective-permute-done
  139.4 2.3 collective-permute-start.2
  141.7 4.5 all-to-all-start
  146.3 0.1 collective-permute-start.3
  146.4 1.6 collective-permute-start.4
  148.1 1.6 collective-permute-done.3
  149.8 1.0 collective-permute-start.5
  150.7 0.8 collective-permute-start.6
  151.5 0.3 dynamic_update_slice.24
  151.8 0.2 dynamic_update_slice.25
  152.0 0.2 dynamic_update_slice.26
  152.2 0.3 dynamic_update_slice.27
  152.5 0.3 dynamic_update_slice.28
  152.8 0.2 dynamic_update_slice.29
  153.0 0.3 collective-permute-done.5
  153.2 0.1 dynamic_update_slice.30
  153.4 1.4 collective-permute-done.6
  154.7 0.3 dynamic_update_slice.31
  155.0 2.4 broadcast_select_fusion.1
  157.4 7.3 %fusion.7 = f32[512,224]{0,1:T(8,128)S(1)} fusion(bf16[512,8192]{1,0:T(8,128)(2,1)} %all-gather.5.cloned.1.call-done, bf16[8192,224]{0,1:T(8,128)(2,1)} %param.14), kind=kOutput, calls=%fused_computation.30 | convolution fusion | flops 1879048192 | bytes 12517376 | tf_op jit(solution)/shard_map/dot_general | solution.py:100
  164.7 0.6 convolution_add_fusion.1
  165.4 1.5 copy-done.7
  166.9 2.7 fusion.10
  169.6 0.7 fusion.1
  170.2 0.5 copy-done.5
  170.7 0.8 fusion.12
  171.5 0.9 select_reduce_fusion
  172.4 0.1 copy.26
  172.5 83.3 %all-reduce.1 = bf16[512,16]{1,0:T(8,128)(2,1)S(1)} all-reduce(f32[512,16]{1,0:T(8,128)S(1)} %copy.26), channel_id=3, replica_groups=mesh['tensor'=8,'adapter'=16] {'tensor','adapter'}, use_global_device_ids=true, to_apply=%region_8.9.clone | all-reduce | flops 8192 | bytes 49152
  255.8 17.2 %all-gather.1 = bf16[16,4,16]{2,1,0:T(4,128)(2,1)S(1)} all-gather(bf16[1,4,16]{2,1,0:T(4,128)(2,1)S(1)} %fusion.4), channel_id=1, replica_groups=mesh['tensor'=8,'adapter'=16] {'adapter'}, dimensions={0}, use_global_device_ids=true | all-gather | bytes 2176 | tf_op jit(solution)/shard_map/all_gather | solution.py:118
  273.1 1.5 convolution_convert_fusion
  274.7 2.4 copy.29
  277.1 8.1 %fusion.11 = f32[512,8192]{1,0:T(8,128)} fusion(bf16[512,224]{0,1:T(8,128)(2,1)S(1)} %fusion.1, bf16[224,8192]{1,0:T(8,128)(2,1)S(1)} %bitcast.36), kind=kOutput, calls=%fused_computation.34 | convolution fusion | flops 1879048192 | bytes 20676608 | tf_op jit(solution)/shard_map/dot_general | solution.py:112
  285.3 0.6 copy-done.9
  285.9 0.6 dynamic-slice.2
  287.1 75.9 %all-reduce.8.cloned.1.call-done = bf16[64,8192]{1,0:T(8,128)(2,1)} async-done(((bf16[64,8192]{1,0:T(8,128)(2,1)}), bf16[64,8192]{1,0:T(8,128)(2,1)}) %all-reduce.8.cloned.1.call-update) | async-done | bytes 1048592
  363.1 222.0 %all-reduce.6.cloned.1.call-done = f32[512,8192]{1,0:T(8,128)} async-done(((f32[512,8192]{1,0:T(8,128)}), f32[512,8192]{1,0:T(8,128)}) %all-reduce.6.cloned.1.call-update) | async-done | bytes 16777232
  585.1 1.7 fusion.2
  (43 shorter events, 0.7 us)
Async XLA Ops:
  6.5 266.6 %copy-start = (bf16[128,8192]{1,0:T(8,128)(2,1)S(1)}, bf16[128,8192]{1,0:T(8,128)(2,1)}, u32[]{:S(2)}) copy-start(bf16[128,8192]{1,0:T(8,128)(2,1)} %param.22) | copy-start | bytes 6291460
  6.5 47.0 %all-gather.7.cloned.1.call-start = ((), (), s32[]{:S(2)}) async-start(), calls=%async_computation.2 | async-start | bytes 1114112 | tf_op jit(solution)/shard_map/all_gather | solution.py:65
  7.3 150.2 %all-gather.5.cloned.1.call-start = ((), (), s32[]{:S(2)}) async-start(), calls=%async_computation.1 | async-start | bytes 9437184 | tf_op jit(solution)/shard_map/all_gather | solution.py:97
  55.7 5.1 copy-start.1
  120.8 18.6 %collective-permute-start = (bf16[64,32]{0,1:T(8,128)(2,1)S(1)}, bf16[64,32]{0,1:T(8,128)(2,1)S(1)}, u32[]{:S(2)}, u32[]{:S(2)}) collective-permute-start(bf16[64,32]{0,1:T(8,128)(2,1)S(1)} %psum.7), channel_id=1, source_target_pairs={{0,16},{16,32},{32,48},{48,64},{64,80},{80,96},{96,112},{112,0},{1... | collective-permute-start | bytes 12296 | tf_op jit(solution)/shard_map/ppermute | solution.py:85
  138.6 7.7 %collective-permute-start.1 = (bf16[64,32]{0,1:T(8,128)(2,1)S(1)}, bf16[64,32]{0,1:T(8,128)(2,1)S(1)}, u32[]{:S(2)}, u32[]{:S(2)}) collective-permute-start(bf16[64,32]{0,1:T(8,128)(2,1)S(1)} %psum.7), channel_id=1, source_target_pairs={{0,112},{16,0},{32,16},{48,32},{64,48},{80,64},{96,80},{112,96},{1... | collective-permute-start | bytes 12296 | tf_op jit(solution)/shard_map/ppermute | solution.py:90
  139.4 7.0 %collective-permute-start.2 = (bf16[64,32]{0,1:T(8,128)(2,1)S(1)}, bf16[64,32]{0,1:T(8,128)(2,1)S(1)}, u32[]{:S(2)}, u32[]{:S(2)}) collective-permute-start(bf16[64,32]{0,1:T(8,128)(2,1)S(1)} %collective-permute-done), channel_id=1, source_target_pairs={{0,16},{16,32},{32,48},{48,64},{64,80},{80,96},{96,112},{112,0},{1... | collective-permute-start | bytes 12296 | tf_op jit(solution)/shard_map/ppermute | solution.py:85
  141.7 133.0 %all-to-all-start = ((bf16[16,224,512]{2,1,0:T(8,128)(2,1)}), bf16[16,224,512]{2,1,0:T(8,128)(2,1)}, u32[]{:S(2)}, u32[]{:S(2)}) async-start(bf16[16,224,512]{2,1,0:T(8,128)(2,1)} %bitcast.38), calls=%async_computation | async-start | bytes 7340032 | tf_op jit(solution)/shard_map/all_to_all | solution.py:111
  146.2 216.9 %all-reduce.8.cloned.1.call-start = ((), (), s32[]{:S(2)}) async-start(), calls=%async_computation.4 | async-start | bytes 2097152
  146.3 3.5 collective-permute-start.3
  146.4 4.3 collective-permute-start.4
  149.8 3.5 collective-permute-start.5
  150.7 4.0 collective-permute-start.6
  157.4 7.3 %copy-start.4 = (bf16[2048,224]{0,1:T(8,128)(2,1)S(1)}, bf16[2048,224]{0,1:T(8,128)(2,1)}, u32[]{:S(2)}) copy-start(bf16[2048,224]{0,1:T(8,128)(2,1)} %param.19) | copy-start | bytes 2752516
  157.4 7.3 %copy-start.2 = (bf16[512,128,16]{0,2,1:T(8,128)(2,1)S(1)}, bf16[512,128,16]{0,2,1:T(8,128)(2,1)}, u32[]{:S(2)}) copy-start(bf16[512,128,16]{0,2,1:T(8,128)(2,1)} %get-tuple-element.7) | copy-start | bytes 6291460
  157.4 8.0 %copy-start.6 = (bf16[512,8192]{1,0:T(8,128)(2,1)S(1)}, bf16[512,8192]{1,0:T(8,128)(2,1)}, u32[]{:S(2)}) copy-start(bf16[512,8192]{1,0:T(8,128)(2,1)} %all-gather.5.cloned.1.call-done) | copy-start | bytes 25165828
  164.7 2.2 copy-start.7
  166.9 2.7 copy-start.3
  166.9 2.7 copy-start.8
  169.5 1.2 copy-start.5
  274.6 310.5 %all-reduce.6.cloned.1.call-start = ((), (), s32[]{:S(2)}) async-start(), calls=%async_computation.3 | async-start | bytes 33554432
  285.2 0.7 copy-start.9
Sparse Core Ops, SparseCore 0:
  9.5 44.0 all-gather.6
  55.8 51.1 all-gather.4
  274.7 88.2 all-reduce.7
  368.4 216.7 all-reduce.5
